TPU v7x, 32 devices: a whole 2x2x4 slice. The times are simulated.
32 devices in a mesh: row: 4 (over y, x), col: 8 (over z, core).
Axes of the slice: x: 2, y: 2, z: 4, core: 2. Of those that a mesh axis runs over, the one named last changes fastest.
Arguments:
- hist_corr: float32 [16384, 16384], P('row', 'col'), may hold values from -1 to 1
- hist_resp: float32 [16384, 16384], P('row', 'col'), may hold values from -1 to 1, as said below
- row_corr: float32 [128, 16384], P(None, 'col'), may hold values from -1 to 1
- row_resp: float32 [128, 16384], P(None, 'col'), may hold values from -1 to 1
Outputs:
- final_corr: float32 [128, 16384], P(None, 'col')
- final_resp: float32 [128, 16384], P(None, 'col')
Inputs may be any that keep to these rules, and one draw needn't show every extreme that they name: hist_resp[s, u] is 0 where u > s and 1 where u == s.
All inputs are finite; a program needn't handle non-finite values.
Results may differ from a plain program's by a relative error of at most 0.00015.
Values sent between devices are 32-bit elements; how exact they have to be, the bound alone decides.
A program may use at most 128 MiB of HBM per device.

v0:
```python
import math
import jax
import jax.numpy as jnp
from jax import lax
from jax.sharding import PartitionSpec as P

HIST = 16384
BLOCKS = 4
step_size = 0.2
heat_reservoir_warmth = 0.6


def turn_rows(values):
    row_count = lax.axis_size("row")
    col_count = lax.axis_size("col")
    my_row = lax.axis_index("row")
    piece_span = values.shape[1] // row_count
    piece = lax.dynamic_slice_in_dim(values, my_row * piece_span, piece_span, 1)
    spread = jnp.broadcast_to(piece[None, None], (col_count, 1) + piece.shape)
    moved = lax.all_to_all(
        lax.all_to_all(spread, "col", split_axis=0, concat_axis=1, tiled=True),
        "row",
        split_axis=1,
        concat_axis=0,
        tiled=True,
    )
    return jnp.transpose(moved, (2, 1, 0, 3)).reshape(piece.shape[0], -1)


def turn_cols(values):
    row_count = lax.axis_size("row")
    col_count = lax.axis_size("col")
    my_col = lax.axis_index("col")
    factor = col_count // row_count
    block_span = values.shape[1] // factor
    piece_span = block_span // col_count
    blocks = values.reshape(values.shape[0], factor, block_span)
    piece = lax.dynamic_slice_in_dim(blocks, my_col * piece_span, piece_span, 2)
    ordered = jnp.transpose(piece, (1, 0, 2))
    spread = jnp.broadcast_to(ordered[None], (row_count,) + ordered.shape)
    moved = lax.all_to_all(
        lax.all_to_all(spread, "row", split_axis=0, concat_axis=1, tiled=True),
        "col",
        split_axis=1,
        concat_axis=0,
        tiled=True,
    )
    return jnp.transpose(moved[:, 0], (1, 0, 2)).reshape(values.shape[0], -1)


def energy_layout(values):
    return turn_rows(values)


def cross_layout(values):
    return turn_cols(values)


def advance(
    autocovariance_curve,
    perturbation_reaction,
    memory_corr,
    memory_resp,
    cross_term,
    norm_enforcing_scalar,
    integration_coefficient,
):
    next_corr = autocovariance_curve + step_size * (
        integration_coefficient * (memory_corr + cross_term)
        - norm_enforcing_scalar * autocovariance_curve
    )
    next_resp = perturbation_reaction + step_size * (
        integration_coefficient * memory_resp - norm_enforcing_scalar * perturbation_reaction
    )
    return (next_corr, next_resp)


def body(hist_corr, hist_resp, row_corr, row_resp):
    highest = lax.Precision.HIGHEST
    integration_coefficient = 1.0 / math.sqrt(HIST)
    autocovariance_curve = row_corr
    perturbation_reaction = row_resp
    for block_index in range(BLOCKS):
        history_integrand = 3.0 * autocovariance_curve * perturbation_reaction
        slope_contribution = 1.5 * autocovariance_curve * autocovariance_curve
        multiplier_terms = jnp.sum(
            history_integrand * autocovariance_curve + slope_contribution * perturbation_reaction,
            axis=1,
        )
        part_cross = lax.dot_general(
            slope_contribution,
            hist_resp,
            (((1,), (1,)), ((), ())),
            precision=highest,
            preferred_element_type=jnp.float32,
        )
        enforcing_scalar_sum = lax.psum(multiplier_terms, "col")
        energy_rows = energy_layout(history_integrand)
        cross_total = lax.psum(part_cross, "col")
        cross_term = cross_layout(cross_total)
        norm_enforcing_scalar = (
            heat_reservoir_warmth + integration_coefficient * enforcing_scalar_sum[:, None]
        )
        part_corr = jnp.dot(
            energy_rows, hist_corr, precision=highest, preferred_element_type=jnp.float32
        )
        part_resp = jnp.dot(
            energy_rows, hist_resp, precision=highest, preferred_element_type=jnp.float32
        )
        memory_corr, memory_resp = lax.psum((part_corr, part_resp), "row")
        autocovariance_curve, perturbation_reaction = advance(
            autocovariance_curve,
            perturbation_reaction,
            memory_corr,
            memory_resp,
            cross_term,
            norm_enforcing_scalar,
            integration_coefficient,
        )
    return (autocovariance_curve, perturbation_reaction)


def solution(mesh):
    in_specs = (P("row", "col"), P("row", "col"), P(None, "col"), P(None, "col"))
    out_specs = (P(None, "col"), P(None, "col"))
    return jax.shard_map(body, mesh=mesh, in_specs=in_specs, out_specs=out_specs, check_vma=False)
```

profile of v0, /device:TPU:0, one launch (start us, length us, event | category | flops | bytes accessed | tf_op | source)
XLA Modules:
  0.0 1180.2 jit_solution(5139241333706496647)
XLA Ops:
  10.2 55.3 %all_to_all.180 = f32[8,1,128,512]{3,2,1,0:T(8,128)} all-to-all(f32[8,1,128,512]{3,2,1,0:T(8,128)S(1)} %broadcast_in_dim.16), channel_id=1, replica_groups=mesh['row'=4,'col'=8] {'col'}, dimensions={0} | all-to-all | bytes 4194304 | tf_op jit(solution)/shard_map/all_to_all | solution.py:21
  65.5 4.6 all-to-all-start.1
  70.1 37.2 %fusion = f32[128,4096]{1,0:T(8,128)S(1)} fusion(f32[4096,2048]{1,0:T(8,128)} %param.5, f32[128,2048]{1,0:T(8,128)S(1)} %copy-done.4), kind=kOutput, calls=%fused_computation.20 | convolution fusion | flops 12885426176 | bytes 36700160 | tf_op jit(solution)/shard_map/dot_general | solution.py:90
  107.4 2.9 reshape.121
  110.3 64.6 %all-reduce.13.cloned.1.call-done = f32[128,2,2048]{2,1,0:T(2,128)} async-done(((f32[128,2,2048]{2,1,0:T(2,128)}), f32[128,2,2048]{2,1,0:T(2,128)}) %all-reduce.13.cloned.1.call-update) | async-done | bytes 2097168 | tf_op jit(solution)/shard_map/psum | solution.py:99
  177.2 4.3 all-to-all-start.2
  183.6 22.4 %fusion.13 = f32[128,2048]{1,0:T(8,128)} fusion(f32[128,4096]{0,1:T(8,128)S(1)} %bitcast.88, f32[4096,2048]{1,0:T(8,128)} %param.5), kind=kOutput, calls=%fused_computation.45 | convolution fusion | flops 12884901888 | bytes 36700160 | tf_op jit(solution)/shard_map/dot_general | solution.py:107
  206.0 22.4 %fusion.12 = f32[128,2048]{1,0:T(8,128)} fusion(f32[128,4096]{0,1:T(8,128)S(1)} %bitcast.89, f32[4096,2048]{1,0:T(8,128)} %param.4), kind=kOutput, calls=%fused_computation.44 | convolution fusion | flops 12884901888 | bytes 36700160 | tf_op jit(solution)/shard_map/dot_general | solution.py:104
  230.8 3.6 all-to-all-start.3
  234.3 29.3 %psum.114 = f32[128]{0:T(128)S(1)} all-reduce(f32[128]{0:T(128)S(1)} %get-tuple-element.20), channel_id=1, replica_groups=mesh['row'=4,'col'=8] {'col'}, use_global_device_ids=true, to_apply=%region_3.0 | all-reduce | flops 128 | bytes 1024 | tf_op jit(solution)/shard_map/psum | solution.py:97
  264.8 33.0 %all-reduce.27.cloned.1.call-done = (f32[128,2048]{1,0:T(8,128)}, f32[128,2048]{1,0:T(8,128)}) async-done(((f32[128,2048]{1,0:T(8,128)}, f32[128,2048]{1,0:T(8,128)}), (f32[128,2048]{1,0:T(8,128)}, f32[128,2048]{1,0:T(8,128)})) %all-reduce.27.cloned.1.call-update) | async-done | bytes 2097168 | tf_op jit(solution)/shard_map/psum | solution.py:110
  297.8 3.0 add_reduce_fusion.2
  301.2 53.5 %all_to_all.181 = f32[8,1,128,512]{3,2,1,0:T(8,128)} all-to-all(f32[8,1,128,512]{3,2,1,0:T(8,128)S(1)} %broadcast_in_dim.18), channel_id=1, replica_groups=mesh['row'=4,'col'=8] {'col'}, dimensions={0} | all-to-all | bytes 4194304 | tf_op jit(solution)/shard_map/all_to_all | solution.py:21
  354.8 4.5 all-to-all-start.5
  359.5 39.0 %fusion.1 = f32[128,4096]{1,0:T(8,128)} fusion(f32[4096,2048]{1,0:T(8,128)} %param.5, f32[128,2048]{1,0:T(8,128)S(1)} %get-tuple-element.18), kind=kOutput, calls=%fused_computation.21 | convolution fusion | flops 12885426176 | bytes 36700160 | tf_op jit(solution)/shard_map/dot_general | solution.py:90
  398.5 4.0 reshape.124
  402.5 64.6 %all-reduce.15.cloned.1.call-done = f32[128,2,2048]{2,1,0:T(2,128)} async-done(((f32[128,2,2048]{2,1,0:T(2,128)}), f32[128,2,2048]{2,1,0:T(2,128)}) %all-reduce.15.cloned.1.call-update) | async-done | bytes 2097168 | tf_op jit(solution)/shard_map/psum | solution.py:99
  469.3 4.3 all-to-all-start.6
  476.0 22.4 %fusion.15 = f32[128,2048]{1,0:T(8,128)} fusion(f32[128,4096]{0,1:T(8,128)S(1)} %bitcast.90, f32[4096,2048]{1,0:T(8,128)} %param.5), kind=kOutput, calls=%fused_computation.47 | convolution fusion | flops 12884901888 | bytes 36700160 | tf_op jit(solution)/shard_map/dot_general | solution.py:107
  498.4 22.4 %fusion.14 = f32[128,2048]{1,0:T(8,128)} fusion(f32[128,4096]{0,1:T(8,128)S(1)} %bitcast.91, f32[4096,2048]{1,0:T(8,128)} %param.4), kind=kOutput, calls=%fused_computation.46 | convolution fusion | flops 12884901888 | bytes 36700160 | tf_op jit(solution)/shard_map/dot_general | solution.py:104
  523.2 3.7 all-to-all-start.7
  526.9 29.3 %psum.118 = f32[128]{0:T(128)S(1)} all-reduce(f32[128]{0:T(128)S(1)} %get-tuple-element.16), channel_id=1, replica_groups=mesh['row'=4,'col'=8] {'col'}, use_global_device_ids=true, to_apply=%region_8.0 | all-reduce | flops 128 | bytes 1024 | tf_op jit(solution)/shard_map/psum | solution.py:97
  557.3 32.9 %all-reduce.25.cloned.1.call-done = (f32[128,2048]{1,0:T(8,128)}, f32[128,2048]{1,0:T(8,128)}) async-done(((f32[128,2048]{1,0:T(8,128)}, f32[128,2048]{1,0:T(8,128)}), (f32[128,2048]{1,0:T(8,128)}, f32[128,2048]{1,0:T(8,128)})) %all-reduce.25.cloned.1.call-update) | async-done | bytes 2097168 | tf_op jit(solution)/shard_map/psum | solution.py:110
  590.2 2.6 add_reduce_fusion.1
  593.9 53.5 %all_to_all.182 = f32[8,1,128,512]{3,2,1,0:T(8,128)} all-to-all(f32[8,1,128,512]{3,2,1,0:T(8,128)S(1)} %broadcast_in_dim.20), channel_id=1, replica_groups=mesh['row'=4,'col'=8] {'col'}, dimensions={0} | all-to-all | bytes 4194304 | tf_op jit(solution)/shard_map/all_to_all | solution.py:21
  647.4 4.5 all-to-all-start.9
  652.1 37.2 %fusion.2 = f32[128,4096]{1,0:T(8,128)S(1)} fusion(f32[4096,2048]{1,0:T(8,128)} %param.5, f32[128,2048]{1,0:T(8,128)S(1)} %get-tuple-element.15), kind=kOutput, calls=%fused_computation.22 | convolution fusion | flops 12885426176 | bytes 36700160 | tf_op jit(solution)/shard_map/dot_general | solution.py:90
  689.3 2.9 reshape.127
  692.2 64.6 %all-reduce.17.cloned.1.call-done = f32[128,2,2048]{2,1,0:T(2,128)} async-done(((f32[128,2,2048]{2,1,0:T(2,128)}), f32[128,2,2048]{2,1,0:T(2,128)}) %all-reduce.17.cloned.1.call-update) | async-done | bytes 2097168 | tf_op jit(solution)/shard_map/psum | solution.py:99
  759.1 4.2 all-to-all-start.10
  765.5 22.4 %fusion.17 = f32[128,2048]{1,0:T(8,128)} fusion(f32[128,4096]{0,1:T(8,128)S(1)} %bitcast.92, f32[4096,2048]{1,0:T(8,128)} %param.5), kind=kOutput, calls=%fused_computation.49 | convolution fusion | flops 12884901888 | bytes 36700160 | tf_op jit(solution)/shard_map/dot_general | solution.py:107
  788.0 22.4 %fusion.16 = f32[128,2048]{1,0:T(8,128)} fusion(f32[128,4096]{0,1:T(8,128)S(1)} %bitcast.93, f32[4096,2048]{1,0:T(8,128)} %param.4), kind=kOutput, calls=%fused_computation.48 | convolution fusion | flops 12884901888 | bytes 36700160 | tf_op jit(solution)/shard_map/dot_general | solution.py:104
  812.7 3.7 all-to-all-start.11
  816.4 29.3 %psum.122 = f32[128]{0:T(128)S(1)} all-reduce(f32[128]{0:T(128)S(1)} %get-tuple-element.13), channel_id=1, replica_groups=mesh['row'=4,'col'=8] {'col'}, use_global_device_ids=true, to_apply=%region_13.0 | all-reduce | flops 128 | bytes 1024 | tf_op jit(solution)/shard_map/psum | solution.py:97
  846.9 32.9 %all-reduce.23.cloned.1.call-done = (f32[128,2048]{1,0:T(8,128)}, f32[128,2048]{1,0:T(8,128)}) async-done(((f32[128,2048]{1,0:T(8,128)}, f32[128,2048]{1,0:T(8,128)}), (f32[128,2048]{1,0:T(8,128)}, f32[128,2048]{1,0:T(8,128)})) %all-reduce.23.cloned.1.call-update) | async-done | bytes 2097168 | tf_op jit(solution)/shard_map/psum | solution.py:110
  879.8 2.6 add_reduce_fusion
  883.4 53.5 %all_to_all.183 = f32[8,1,128,512]{3,2,1,0:T(8,128)} all-to-all(f32[8,1,128,512]{3,2,1,0:T(8,128)S(1)} %broadcast_in_dim.22), channel_id=1, replica_groups=mesh['row'=4,'col'=8] {'col'}, dimensions={0} | all-to-all | bytes 4194304 | tf_op jit(solution)/shard_map/all_to_all | solution.py:21
  936.9 4.5 all-to-all-start.13
  941.9 37.3 %fusion.3 = f32[128,4096]{1,0:T(8,128)S(1)} fusion(f32[4096,2048]{1,0:T(8,128)} %param.5, f32[128,2048]{1,0:T(8,128)S(1)} %get-tuple-element.12), kind=kOutput, calls=%fused_computation.23 | convolution fusion | flops 12885426176 | bytes 36700160 | tf_op jit(solution)/shard_map/dot_general | solution.py:90
  979.1 2.9 reshape.130
  982.0 64.6 %all-reduce.19.cloned.1.call-done = f32[128,2,2048]{2,1,0:T(2,128)} async-done(((f32[128,2,2048]{2,1,0:T(2,128)}), f32[128,2,2048]{2,1,0:T(2,128)}) %all-reduce.19.cloned.1.call-update) | async-done | bytes 2097168 | tf_op jit(solution)/shard_map/psum | solution.py:99
  1048.8 3.6 all-to-all-start.14
  1054.6 22.4 %fusion.19 = f32[128,2048]{1,0:T(8,128)} fusion(f32[128,4096]{0,1:T(8,128)S(1)} %bitcast.94, f32[4096,2048]{1,0:T(8,128)} %param.5), kind=kOutput, calls=%fused_computation.51 | convolution fusion | flops 12884901888 | bytes 36700160 | tf_op jit(solution)/shard_map/dot_general | solution.py:107
  1077.0 22.4 %fusion.18 = f32[128,2048]{1,0:T(8,128)} fusion(f32[128,4096]{0,1:T(8,128)S(1)} %bitcast.95, f32[4096,2048]{1,0:T(8,128)} %param.4), kind=kOutput, calls=%fused_computation.50 | convolution fusion | flops 12884901888 | bytes 36700160 | tf_op jit(solution)/shard_map/dot_general | solution.py:104
  1100.6 3.7 all-to-all-start.15
  1104.3 29.3 %psum.126 = f32[128]{0:T(128)S(1)} all-reduce(f32[128]{0:T(128)S(1)} %get-tuple-element.10), channel_id=1, replica_groups=mesh['row'=4,'col'=8] {'col'}, use_global_device_ids=true, to_apply=%region_18.0 | all-reduce | flops 128 | bytes 1024 | tf_op jit(solution)/shard_map/psum | solution.py:97
  1134.7 34.2 %all-reduce.21.cloned.1.call-done = (f32[128,2048]{1,0:T(8,128)}, f32[128,2048]{1,0:T(8,128)}) async-done(((f32[128,2048]{1,0:T(8,128)}, f32[128,2048]{1,0:T(8,128)}), (f32[128,2048]{1,0:T(8,128)}, f32[128,2048]{1,0:T(8,128)})) %all-reduce.21.cloned.1.call-update) | async-done | bytes 2097168 | tf_op jit(solution)/shard_map/psum | solution.py:110
  1168.9 3.7 multiply_add_fusion
  (82 shorter events, 35.7 us)
Async XLA Ops:
  65.5 4.7 copy-start.4
  65.5 110.4 %all-to-all-start.1 = ((f32[1,8,128,512]{3,2,0,1:T(8,128)}), f32[1,8,128,512]{3,2,0,1:T(8,128)}, u32[]{:S(2)}, u32[]{:S(2)}) async-start(f32[1,8,128,512]{3,2,0,1:T(8,128)} %bitcast.1), calls=%async_computation.1 | async-start | bytes 4194304 | tf_op jit(solution)/shard_map/all_to_all | solution.py:20
  70.1 104.8 %all-reduce.13.cloned.1.call-start = ((), (), s32[]{:S(2)}) async-start(), calls=%async_computation.16 | async-start | bytes 4194304 | tf_op jit(solution)/shard_map/psum | solution.py:99
  177.2 51.3 %all-to-all-start.2 = ((f32[4,2,128,256]{3,1,2,0:T(2,128)}), f32[4,2,128,256]{3,1,2,0:T(2,128)}, u32[]{:S(2)}, u32[]{:S(2)}) async-start(f32[4,2,128,256]{3,1,2,0:T(2,128)} %broadcast_in_dim.17), calls=%async_computation.2 | async-start | bytes 2097152 | tf_op jit(solution)/shard_map/all_to_all | solution.py:42
  181.4 116.4 %all-reduce.27.cloned.1.call-start = ((), (), s32[]{:S(2)}) async-start(), calls=%async_computation.23 | async-start | bytes 4194304 | tf_op jit(solution)/shard_map/psum | solution.py:110
  230.8 32.9 %all-to-all-start.3 = ((f32[1,8,128,256]{3,2,0,1:T(8,128)}), f32[1,8,128,256]{3,2,0,1:T(8,128)S(1)}, u32[]{:S(2)}, u32[]{:S(2)}) async-start(f32[1,8,128,256]{3,2,0,1:T(8,128)} %bitcast.7), calls=%async_computation.3 | async-start | bytes 2097152 | tf_op jit(solution)/shard_map/all_to_all | solution.py:41
  300.8 58.7 %copy-start = (f32[128,2048]{1,0:T(8,128)}, f32[128,2048]{1,0:T(8,128)S(1)}, u32[]{:S(2)}) copy-start(f32[128,2048]{1,0:T(8,128)S(1)} %get-tuple-element.18) | copy-start | bytes 3145732
  354.8 113.3 %all-to-all-start.5 = ((f32[1,8,128,512]{3,2,0,1:T(8,128)}), f32[1,8,128,512]{3,2,0,1:T(8,128)}, u32[]{:S(2)}, u32[]{:S(2)}) async-start(f32[1,8,128,512]{3,2,0,1:T(8,128)} %bitcast.96), calls=%async_computation.5 | async-start | bytes 4194304 | tf_op jit(solution)/shard_map/all_to_all | solution.py:20
  359.2 107.9 %all-reduce.15.cloned.1.call-start = ((), (), s32[]{:S(2)}) async-start(), calls=%async_computation.17 | async-start | bytes 4194304 | tf_op jit(solution)/shard_map/psum | solution.py:99
  469.3 51.5 %all-to-all-start.6 = ((f32[4,2,128,256]{3,1,2,0:T(2,128)}), f32[4,2,128,256]{3,1,2,0:T(2,128)}, u32[]{:S(2)}, u32[]{:S(2)}) async-start(f32[4,2,128,256]{3,1,2,0:T(2,128)} %broadcast_in_dim.19), calls=%async_computation.6 | async-start | bytes 2097152 | tf_op jit(solution)/shard_map/all_to_all | solution.py:42
  473.6 116.6 %all-reduce.25.cloned.1.call-start = ((), (), s32[]{:S(2)}) async-start(), calls=%async_computation.22 | async-start | bytes 4194304 | tf_op jit(solution)/shard_map/psum | solution.py:110
  523.2 67.0 %copy-start.1 = (f32[128,2048]{1,0:T(8,128)S(1)}, f32[128,2048]{1,0:T(8,128)}, u32[]{:S(2)}) copy-start(f32[128,2048]{1,0:T(8,128)} %copy-done) | copy-start | bytes 3145732
  523.2 33.0 %all-to-all-start.7 = ((f32[1,8,128,256]{3,2,0,1:T(8,128)}), f32[1,8,128,256]{3,2,0,1:T(8,128)S(1)}, u32[]{:S(2)}, u32[]{:S(2)}) async-start(f32[1,8,128,256]{3,2,0,1:T(8,128)} %bitcast.101), calls=%async_computation.7 | async-start | bytes 2097152 | tf_op jit(solution)/shard_map/all_to_all | solution.py:41
  592.9 1.0 copy-start.5
  647.4 110.4 %all-to-all-start.9 = ((f32[1,8,128,512]{3,2,0,1:T(8,128)}), f32[1,8,128,512]{3,2,0,1:T(8,128)}, u32[]{:S(2)}, u32[]{:S(2)}) async-start(f32[1,8,128,512]{3,2,0,1:T(8,128)} %bitcast.21), calls=%async_computation.9 | async-start | bytes 4194304 | tf_op jit(solution)/shard_map/all_to_all | solution.py:20
  651.8 105.0 %all-reduce.17.cloned.1.call-start = ((), (), s32[]{:S(2)}) async-start(), calls=%async_computation.18 | async-start | bytes 4194304 | tf_op jit(solution)/shard_map/psum | solution.py:99
  759.1 51.3 %all-to-all-start.10 = ((f32[4,2,128,256]{3,1,2,0:T(2,128)}), f32[4,2,128,256]{3,1,2,0:T(2,128)}, u32[]{:S(2)}, u32[]{:S(2)}) async-start(f32[4,2,128,256]{3,1,2,0:T(2,128)} %broadcast_in_dim.21), calls=%async_computation.10 | async-start | bytes 2097152 | tf_op jit(solution)/shard_map/all_to_all | solution.py:42
  763.3 116.5 %all-reduce.23.cloned.1.call-start = ((), (), s32[]{:S(2)}) async-start(), calls=%async_computation.21 | async-start | bytes 4194304 | tf_op jit(solution)/shard_map/psum | solution.py:110
  812.7 67.0 %copy-start.6 = (f32[128,2048]{1,0:T(8,128)S(1)}, f32[128,2048]{1,0:T(8,128)}, u32[]{:S(2)}) copy-start(f32[128,2048]{1,0:T(8,128)} %copy-done.5) | copy-start | bytes 3145732
  812.7 33.0 %all-to-all-start.11 = ((f32[1,8,128,256]{3,2,0,1:T(8,128)}), f32[1,8,128,256]{3,2,0,1:T(8,128)S(1)}, u32[]{:S(2)}, u32[]{:S(2)}) async-start(f32[1,8,128,256]{3,2,0,1:T(8,128)} %bitcast.102), calls=%async_computation.11 | async-start | bytes 2097152 | tf_op jit(solution)/shard_map/all_to_all | solution.py:41
  882.4 1.0 copy-start.7
  882.4 59.4 %copy-start.2 = (f32[128,2048]{1,0:T(8,128)}, f32[128,2048]{1,0:T(8,128)S(1)}, u32[]{:S(2)}) copy-start(f32[128,2048]{1,0:T(8,128)S(1)} %get-tuple-element.12) | copy-start | bytes 3145732
  936.9 110.6 %all-to-all-start.13 = ((f32[1,8,128,512]{3,2,0,1:T(8,128)}), f32[1,8,128,512]{3,2,0,1:T(8,128)}, u32[]{:S(2)}, u32[]{:S(2)}) async-start(f32[1,8,128,512]{3,2,0,1:T(8,128)} %bitcast.31), calls=%async_computation.13 | async-start | bytes 4194304 | tf_op jit(solution)/shard_map/all_to_all | solution.py:20
  941.4 105.2 %all-reduce.19.cloned.1.call-start = ((), (), s32[]{:S(2)}) async-start(), calls=%async_computation.19 | async-start | bytes 4194304 | tf_op jit(solution)/shard_map/psum | solution.py:99
  1048.8 50.7 %all-to-all-start.14 = ((f32[4,2,128,256]{3,1,2,0:T(2,128)}), f32[4,2,128,256]{3,1,2,0:T(2,128)S(1)}, u32[]{:S(2)}, u32[]{:S(2)}) async-start(f32[4,2,128,256]{3,1,2,0:T(2,128)} %broadcast_in_dim.23), calls=%async_computation.14 | async-start | bytes 2097152 | tf_op jit(solution)/shard_map/all_to_all | solution.py:42
  1052.5 116.5 %all-reduce.21.cloned.1.call-start = ((), (), s32[]{:S(2)}) async-start(), calls=%async_computation.20 | async-start | bytes 4194304 | tf_op jit(solution)/shard_map/psum | solution.py:110
  1100.6 68.4 %copy-start.3 = (f32[128,2048]{1,0:T(8,128)S(1)}, f32[128,2048]{1,0:T(8,128)}, u32[]{:S(2)}) copy-start(f32[128,2048]{1,0:T(8,128)} %copy-done.2) | copy-start | bytes 3145732
  1100.6 68.4 %copy-start.8 = (f32[128,2048]{1,0:T(8,128)S(1)}, f32[128,2048]{1,0:T(8,128)}, u32[]{:S(2)}) copy-start(f32[128,2048]{1,0:T(8,128)} %copy-done.7) | copy-start | bytes 3145732
  1100.6 33.0 %all-to-all-start.15 = ((f32[1,8,128,256]{3,2,0,1:T(8,128)}), f32[1,8,128,256]{3,2,0,1:T(8,128)S(1)}, u32[]{:S(2)}, u32[]{:S(2)}) async-start(f32[1,8,128,256]{3,2,0,1:T(8,128)} %bitcast.103), calls=%async_computation.15 | async-start | bytes 2097152 | tf_op jit(solution)/shard_map/all_to_all | solution.py:41
Sparse Core Ops, SparseCore 0:
  110.4 64.4 all-reduce.12
  402.6 64.4 all-reduce.14
  692.3 64.4 all-reduce.16
  982.1 64.4 all-reduce.18
Sparse Core Ops, SparseCore 1:
  228.5 69.2 all-reduce.26
  521.0 69.2 all-reduce.24
  810.5 69.2 all-reduce.22
  1099.6 69.3 all-reduce.20
where the time goes:
time: 1190 us; the launch traced here: 1180 us
  waiting for transfers between devices  392 us (33%)
  blocking collectives  333 us (28%)
  matrix products  330 us (28%)
  starting transfers between devices  51 us (4%)
  local copies, waits for them, and re-layouts  43.7 us (4%)
  between operations  16.1 us (1%)
  other arithmetic  14.3 us (1%)
    psum x4, waiting for transfers between devices, body(): cross_total = lax.psum(part_cross, 'col')  258 us
    all_to_all x4, blocking collectives, turn_rows(): lax.all_to_all(spread, 'col', split_axis=0, concat_axis=1, tiled=True)  216 us
    dot_general x4, matrix products, body(): lax.dot_general(slope_contribution, hist_resp, (((1,), (1,)), ((), ())),...  151 us
    psum x4, waiting for transfers between devices, body(): memory_corr, memory_resp = lax.psum((part_corr, part_resp), 'row')  133 us
    psum x4, blocking collectives, body(): enforcing_scalar_sum = lax.psum(multiplier_terms, 'col')  117 us
    dot_general x4, matrix products, body(): jnp.dot(energy_rows, hist_resp, precision=highest, preferred_element_type...  89.7 us
    dot_general x4, matrix products, body(): jnp.dot(energy_rows, hist_corr, precision=highest, preferred_element_type...  89.7 us
  transfers between devices with their start and end apart: 20, of which 8 were waited for; matrix products, arithmetic and copies ran while one was open for 31% of the time, Pallas kernels for 0%

commit v1 on v0

--- a/solution.py
+++ b/solution.py
@@ -94,7 +94,7 @@
             precision=highest,
             preferred_element_type=jnp.float32,
         )
-        enforcing_scalar_sum = lax.psum(multiplier_terms, "col")
+        enforcing_scalar_sum = jnp.sum(lax.all_gather(multiplier_terms, "col"), axis=0)
         energy_rows = energy_layout(history_integrand)
         cross_total = lax.psum(part_cross, "col")
         cross_term = cross_layout(cross_total)

time: 1190 us -> 1190 us (level)
  blocking collectives: 333 us -> 315 us
  waiting for transfers between devices: 392 us -> 410 us
    psum x4 -> x0, blocking collectives: 117 us -> none  [body(): enforcing_scalar_sum = lax.psum(multiplier_terms, 'col')]
    all_gather x0 -> x4, blocking collectives: none -> 98.6 us  [body(): lax.all_gather(multiplier_terms, 'col')]
  transfers between devices with their start and end apart: 20 -> 20, of which waited for: 8 -> 12; matrix products, arithmetic and copies ran while one was open for 31% -> 31% of each run, Pallas kernels for 0% -> 0%
where the time goes in v1:
time: 1190 us; the launch traced here: 1180 us
  waiting for transfers between devices  410 us (34%)
  matrix products  330 us (28%)
  blocking collectives  315 us (26%)
  starting transfers between devices  51 us (4%)
  local copies, waits for them, and re-layouts  43.7 us (4%)
  between operations  16.1 us (1%)
  other arithmetic  14.4 us (1%)
    psum x4, waiting for transfers between devices, body(): cross_total = lax.psum(part_cross, 'col')  259 us
    all_to_all x4, blocking collectives, turn_rows(): lax.all_to_all(spread, 'col', split_axis=0, concat_axis=1, tiled=True)  216 us
    dot_general x4, matrix products, body(): lax.dot_general(slope_contribution, hist_resp, (((1,), (1,)), ((), ())),...  151 us
    psum x4, waiting for transfers between devices, body(): memory_corr, memory_resp = lax.psum((part_corr, part_resp), 'row')  144 us
    all_gather x4, blocking collectives, body(): lax.all_gather(multiplier_terms, 'col')  98.6 us
    dot_general x4, matrix products, body(): jnp.dot(energy_rows, hist_resp, precision=highest, preferred_element_type...  89.7 us
    dot_general x4, matrix products, body(): jnp.dot(energy_rows, hist_corr, precision=highest, preferred_element_type...  89.7 us
  transfers between devices with their start and end apart: 20, of which 12 were waited for; matrix products, arithmetic and copies ran while one was open for 31% of the time, Pallas kernels for 0%

profile of v1, /device:TPU:0, one launch (start us, length us, event | category | flops | bytes accessed | tf_op | source)
XLA Modules:
  0.0 1180.3 jit_solution(17961527713946366073)
XLA Ops:
  10.2 55.3 %all_to_all.180 = f32[8,1,128,512]{3,2,1,0:T(8,128)} all-to-all(f32[8,1,128,512]{3,2,1,0:T(8,128)S(1)} %broadcast_in_dim.16), channel_id=1, replica_groups=mesh['row'=4,'col'=8] {'col'}, dimensions={0} | all-to-all | bytes 4194304 | tf_op jit(solution)/shard_map/all_to_all | solution.py:21
  65.5 4.6 all-to-all-start.1
  70.1 37.2 %fusion = f32[128,4096]{1,0:T(8,128)S(1)} fusion(f32[4096,2048]{1,0:T(8,128)} %param.5, f32[128,2048]{1,0:T(8,128)S(1)} %copy-done.4), kind=kOutput, calls=%fused_computation.20 | convolution fusion | flops 12885426176 | bytes 36700160 | tf_op jit(solution)/shard_map/dot_general | solution.py:90
  107.4 2.9 reshape.133
  110.3 64.6 %all-reduce.13.cloned.1.call-done = f32[128,2,2048]{2,1,0:T(2,128)} async-done(((f32[128,2,2048]{2,1,0:T(2,128)}), f32[128,2,2048]{2,1,0:T(2,128)}) %all-reduce.13.cloned.1.call-update) | async-done | bytes 2097168 | tf_op jit(solution)/shard_map/psum | solution.py:99
  177.2 4.3 all-to-all-start.2
  183.6 22.4 %fusion.13 = f32[128,2048]{1,0:T(8,128)} fusion(f32[128,4096]{0,1:T(8,128)S(1)} %bitcast.92, f32[4096,2048]{1,0:T(8,128)} %param.5), kind=kOutput, calls=%fused_computation.45 | convolution fusion | flops 12884901888 | bytes 36700160 | tf_op jit(solution)/shard_map/dot_general | solution.py:107
  206.0 22.4 %fusion.12 = f32[128,2048]{1,0:T(8,128)} fusion(f32[128,4096]{0,1:T(8,128)S(1)} %bitcast.93, f32[4096,2048]{1,0:T(8,128)} %param.4), kind=kOutput, calls=%fused_computation.44 | convolution fusion | flops 12884901888 | bytes 36700160 | tf_op jit(solution)/shard_map/dot_general | solution.py:104
  230.8 3.6 all-to-all-start.3
  234.3 24.7 %all-gather.4 = f32[8,1,128]{2,1,0:T(1,128)S(1)} all-gather(f32[1,1,128]{2,1,0:T(1,128)S(1)} %bitcast.115), channel_id=2, replica_groups=mesh['row'=4,'col'=8] {'col'}, dimensions={0}, use_global_device_ids=true | all-gather | bytes 4608 | tf_op jit(solution)/shard_map/all_gather | solution.py:97
  261.9 35.9 %all-reduce.27.cloned.1.call-done = (f32[128,2048]{1,0:T(8,128)}, f32[128,2048]{1,0:T(8,128)}) async-done(((f32[128,2048]{1,0:T(8,128)}, f32[128,2048]{1,0:T(8,128)}), (f32[128,2048]{1,0:T(8,128)}, f32[128,2048]{1,0:T(8,128)})) %all-reduce.27.cloned.1.call-update) | async-done | bytes 2097168 | tf_op jit(solution)/shard_map/psum | solution.py:110
  297.8 3.0 add_reduce_fusion.2
  301.2 53.5 %all_to_all.181 = f32[8,1,128,512]{3,2,1,0:T(8,128)} all-to-all(f32[8,1,128,512]{3,2,1,0:T(8,128)S(1)} %broadcast_in_dim.18), channel_id=1, replica_groups=mesh['row'=4,'col'=8] {'col'}, dimensions={0} | all-to-all | bytes 4194304 | tf_op jit(solution)/shard_map/all_to_all | solution.py:21
  354.8 4.5 all-to-all-start.5
  359.5 39.0 %fusion.1 = f32[128,4096]{1,0:T(8,128)} fusion(f32[4096,2048]{1,0:T(8,128)} %param.5, f32[128,2048]{1,0:T(8,128)S(1)} %get-tuple-element.18), kind=kOutput, calls=%fused_computation.21 | convolution fusion | flops 12885426176 | bytes 36700160 | tf_op jit(solution)/shard_map/dot_general | solution.py:90
  398.4 4.0 reshape.136
  402.5 64.6 %all-reduce.15.cloned.1.call-done = f32[128,2,2048]{2,1,0:T(2,128)} async-done(((f32[128,2,2048]{2,1,0:T(2,128)}), f32[128,2,2048]{2,1,0:T(2,128)}) %all-reduce.15.cloned.1.call-update) | async-done | bytes 2097168 | tf_op jit(solution)/shard_map/psum | solution.py:99
  469.3 4.3 all-to-all-start.6
  476.0 22.4 %fusion.15 = f32[128,2048]{1,0:T(8,128)} fusion(f32[128,4096]{0,1:T(8,128)S(1)} %bitcast.94, f32[4096,2048]{1,0:T(8,128)} %param.5), kind=kOutput, calls=%fused_computation.47 | convolution fusion | flops 12884901888 | bytes 36700160 | tf_op jit(solution)/shard_map/dot_general | solution.py:107
  498.4 22.4 %fusion.14 = f32[128,2048]{1,0:T(8,128)} fusion(f32[128,4096]{0,1:T(8,128)S(1)} %bitcast.95, f32[4096,2048]{1,0:T(8,128)} %param.4), kind=kOutput, calls=%fused_computation.46 | convolution fusion | flops 12884901888 | bytes 36700160 | tf_op jit(solution)/shard_map/dot_general | solution.py:104
  523.2 3.7 all-to-all-start.7
  526.9 24.7 %all-gather.5 = f32[8,1,128]{2,1,0:T(1,128)S(1)} all-gather(f32[1,1,128]{2,1,0:T(1,128)S(1)} %bitcast.114), channel_id=3, replica_groups=mesh['row'=4,'col'=8] {'col'}, dimensions={0}, use_global_device_ids=true | all-gather | bytes 4608 | tf_op jit(solution)/shard_map/all_gather | solution.py:97
  554.5 35.7 %all-reduce.25.cloned.1.call-done = (f32[128,2048]{1,0:T(8,128)}, f32[128,2048]{1,0:T(8,128)}) async-done(((f32[128,2048]{1,0:T(8,128)}, f32[128,2048]{1,0:T(8,128)}), (f32[128,2048]{1,0:T(8,128)}, f32[128,2048]{1,0:T(8,128)})) %all-reduce.25.cloned.1.call-update) | async-done | bytes 2097168 | tf_op jit(solution)/shard_map/psum | solution.py:110
  590.2 2.6 add_reduce_fusion.1
  593.8 53.5 %all_to_all.182 = f32[8,1,128,512]{3,2,1,0:T(8,128)} all-to-all(f32[8,1,128,512]{3,2,1,0:T(8,128)S(1)} %broadcast_in_dim.20), channel_id=1, replica_groups=mesh['row'=4,'col'=8] {'col'}, dimensions={0} | all-to-all | bytes 4194304 | tf_op jit(solution)/shard_map/all_to_all | solution.py:21
  647.4 4.5 all-to-all-start.9
  652.1 37.2 %fusion.2 = f32[128,4096]{1,0:T(8,128)S(1)} fusion(f32[4096,2048]{1,0:T(8,128)} %param.5, f32[128,2048]{1,0:T(8,128)S(1)} %get-tuple-element.15), kind=kOutput, calls=%fused_computation.22 | convolution fusion | flops 12885426176 | bytes 36700160 | tf_op jit(solution)/shard_map/dot_general | solution.py:90
  689.3 2.9 reshape.139
  692.2 64.7 %all-reduce.17.cloned.1.call-done = f32[128,2,2048]{2,1,0:T(2,128)} async-done(((f32[128,2,2048]{2,1,0:T(2,128)}), f32[128,2,2048]{2,1,0:T(2,128)}) %all-reduce.17.cloned.1.call-update) | async-done | bytes 2097168 | tf_op jit(solution)/shard_map/psum | solution.py:99
  759.1 4.2 all-to-all-start.10
  765.6 22.4 %fusion.17 = f32[128,2048]{1,0:T(8,128)} fusion(f32[128,4096]{0,1:T(8,128)S(1)} %bitcast.96, f32[4096,2048]{1,0:T(8,128)} %param.5), kind=kOutput, calls=%fused_computation.49 | convolution fusion | flops 12884901888 | bytes 36700160 | tf_op jit(solution)/shard_map/dot_general | solution.py:107
  788.0 22.4 %fusion.16 = f32[128,2048]{1,0:T(8,128)} fusion(f32[128,4096]{0,1:T(8,128)S(1)} %bitcast.97, f32[4096,2048]{1,0:T(8,128)} %param.4), kind=kOutput, calls=%fused_computation.48 | convolution fusion | flops 12884901888 | bytes 36700160 | tf_op jit(solution)/shard_map/dot_general | solution.py:104
  812.8 3.7 all-to-all-start.11
  816.5 24.7 %all-gather.6 = f32[8,1,128]{2,1,0:T(1,128)S(1)} all-gather(f32[1,1,128]{2,1,0:T(1,128)S(1)} %bitcast.113), channel_id=4, replica_groups=mesh['row'=4,'col'=8] {'col'}, dimensions={0}, use_global_device_ids=true | all-gather | bytes 4608 | tf_op jit(solution)/shard_map/all_gather | solution.py:97
  844.1 35.7 %all-reduce.23.cloned.1.call-done = (f32[128,2048]{1,0:T(8,128)}, f32[128,2048]{1,0:T(8,128)}) async-done(((f32[128,2048]{1,0:T(8,128)}, f32[128,2048]{1,0:T(8,128)}), (f32[128,2048]{1,0:T(8,128)}, f32[128,2048]{1,0:T(8,128)})) %all-reduce.23.cloned.1.call-update) | async-done | bytes 2097168 | tf_op jit(solution)/shard_map/psum | solution.py:110
  879.8 2.6 add_reduce_fusion
  883.4 53.5 %all_to_all.183 = f32[8,1,128,512]{3,2,1,0:T(8,128)} all-to-all(f32[8,1,128,512]{3,2,1,0:T(8,128)S(1)} %broadcast_in_dim.22), channel_id=1, replica_groups=mesh['row'=4,'col'=8] {'col'}, dimensions={0} | all-to-all | bytes 4194304 | tf_op jit(solution)/shard_map/all_to_all | solution.py:21
  936.9 4.5 all-to-all-start.13
  941.9 37.2 %fusion.3 = f32[128,4096]{1,0:T(8,128)S(1)} fusion(f32[4096,2048]{1,0:T(8,128)} %param.5, f32[128,2048]{1,0:T(8,128)S(1)} %get-tuple-element.12), kind=kOutput, calls=%fused_computation.23 | convolution fusion | flops 12885426176 | bytes 36700160 | tf_op jit(solution)/shard_map/dot_general | solution.py:90
  979.1 2.9 reshape.142
  982.0 64.7 %all-reduce.19.cloned.1.call-done = f32[128,2,2048]{2,1,0:T(2,128)} async-done(((f32[128,2,2048]{2,1,0:T(2,128)}), f32[128,2,2048]{2,1,0:T(2,128)}) %all-reduce.19.cloned.1.call-update) | async-done | bytes 2097168 | tf_op jit(solution)/shard_map/psum | solution.py:99
  1048.9 3.6 all-to-all-start.14
  1054.7 22.4 %fusion.19 = f32[128,2048]{1,0:T(8,128)} fusion(f32[128,4096]{0,1:T(8,128)S(1)} %bitcast.98, f32[4096,2048]{1,0:T(8,128)} %param.5), kind=kOutput, calls=%fused_computation.51 | convolution fusion | flops 12884901888 | bytes 36700160 | tf_op jit(solution)/shard_map/dot_general | solution.py:107
  1077.1 22.4 %fusion.18 = f32[128,2048]{1,0:T(8,128)} fusion(f32[128,4096]{0,1:T(8,128)S(1)} %bitcast.99, f32[4096,2048]{1,0:T(8,128)} %param.4), kind=kOutput, calls=%fused_computation.50 | convolution fusion | flops 12884901888 | bytes 36700160 | tf_op jit(solution)/shard_map/dot_general | solution.py:104
  1100.7 3.7 all-to-all-start.15
  1104.3 24.7 %all-gather.7 = f32[8,1,128]{2,1,0:T(1,128)S(1)} all-gather(f32[1,1,128]{2,1,0:T(1,128)S(1)} %bitcast.112), channel_id=5, replica_groups=mesh['row'=4,'col'=8] {'col'}, dimensions={0}, use_global_device_ids=true | all-gather | bytes 4608 | tf_op jit(solution)/shard_map/all_gather | solution.py:97
  1131.9 37.1 %all-reduce.21.cloned.1.call-done = (f32[128,2048]{1,0:T(8,128)}, f32[128,2048]{1,0:T(8,128)}) async-done(((f32[128,2048]{1,0:T(8,128)}, f32[128,2048]{1,0:T(8,128)}), (f32[128,2048]{1,0:T(8,128)}, f32[128,2048]{1,0:T(8,128)})) %all-reduce.21.cloned.1.call-update) | async-done | bytes 2097168 | tf_op jit(solution)/shard_map/psum | solution.py:110
  1169.0 3.7 multiply_add_fusion
  (86 shorter events, 43.1 us)
Async XLA Ops:
  65.5 4.7 copy-start.4
  65.5 110.4 %all-to-all-start.1 = ((f32[1,8,128,512]{3,2,0,1:T(8,128)}), f32[1,8,128,512]{3,2,0,1:T(8,128)}, u32[]{:S(2)}, u32[]{:S(2)}) async-start(f32[1,8,128,512]{3,2,0,1:T(8,128)} %bitcast.1), calls=%async_computation.1 | async-start | bytes 4194304 | tf_op jit(solution)/shard_map/all_to_all | solution.py:20
  70.1 104.8 %all-reduce.13.cloned.1.call-start = ((), (), s32[]{:S(2)}) async-start(), calls=%async_computation.16 | async-start | bytes 4194304 | tf_op jit(solution)/shard_map/psum | solution.py:99
  177.2 51.3 %all-to-all-start.2 = ((f32[4,2,128,256]{3,1,2,0:T(2,128)}), f32[4,2,128,256]{3,1,2,0:T(2,128)}, u32[]{:S(2)}, u32[]{:S(2)}) async-start(f32[4,2,128,256]{3,1,2,0:T(2,128)} %broadcast_in_dim.17), calls=%async_computation.2 | async-start | bytes 2097152 | tf_op jit(solution)/shard_map/all_to_all | solution.py:42
  181.4 116.4 %all-reduce.27.cloned.1.call-start = ((), (), s32[]{:S(2)}) async-start(), calls=%async_computation.23 | async-start | bytes 4194304 | tf_op jit(solution)/shard_map/psum | solution.py:110
  230.8 30.1 %all-to-all-start.3 = ((f32[1,8,128,256]{3,2,0,1:T(8,128)}), f32[1,8,128,256]{3,2,0,1:T(8,128)S(1)}, u32[]{:S(2)}, u32[]{:S(2)}) async-start(f32[1,8,128,256]{3,2,0,1:T(8,128)} %bitcast.7), calls=%async_computation.3 | async-start | bytes 2097152 | tf_op jit(solution)/shard_map/all_to_all | solution.py:41
  300.8 58.7 %copy-start = (f32[128,2048]{1,0:T(8,128)}, f32[128,2048]{1,0:T(8,128)S(1)}, u32[]{:S(2)}) copy-start(f32[128,2048]{1,0:T(8,128)S(1)} %get-tuple-element.18) | copy-start | bytes 3145732
  354.8 113.3 %all-to-all-start.5 = ((f32[1,8,128,512]{3,2,0,1:T(8,128)}), f32[1,8,128,512]{3,2,0,1:T(8,128)}, u32[]{:S(2)}, u32[]{:S(2)}) async-start(f32[1,8,128,512]{3,2,0,1:T(8,128)} %bitcast.100), calls=%async_computation.5 | async-start | bytes 4194304 | tf_op jit(solution)/shard_map/all_to_all | solution.py:20
  359.2 107.9 %all-reduce.15.cloned.1.call-start = ((), (), s32[]{:S(2)}) async-start(), calls=%async_computation.17 | async-start | bytes 4194304 | tf_op jit(solution)/shard_map/psum | solution.py:99
  469.3 51.5 %all-to-all-start.6 = ((f32[4,2,128,256]{3,1,2,0:T(2,128)}), f32[4,2,128,256]{3,1,2,0:T(2,128)}, u32[]{:S(2)}, u32[]{:S(2)}) async-start(f32[4,2,128,256]{3,1,2,0:T(2,128)} %broadcast_in_dim.19), calls=%async_computation.6 | async-start | bytes 2097152 | tf_op jit(solution)/shard_map/all_to_all | solution.py:42
  473.6 116.6 %all-reduce.25.cloned.1.call-start = ((), (), s32[]{:S(2)}) async-start(), calls=%async_computation.22 | async-start | bytes 4194304 | tf_op jit(solution)/shard_map/psum | solution.py:110
  523.2 67.0 %copy-start.1 = (f32[128,2048]{1,0:T(8,128)S(1)}, f32[128,2048]{1,0:T(8,128)}, u32[]{:S(2)}) copy-start(f32[128,2048]{1,0:T(8,128)} %copy-done) | copy-start | bytes 3145732
  523.2 30.2 %all-to-all-start.7 = ((f32[1,8,128,256]{3,2,0,1:T(8,128)}), f32[1,8,128,256]{3,2,0,1:T(8,128)S(1)}, u32[]{:S(2)}, u32[]{:S(2)}) async-start(f32[1,8,128,256]{3,2,0,1:T(8,128)} %bitcast.106), calls=%async_computation.7 | async-start | bytes 2097152 | tf_op jit(solution)/shard_map/all_to_all | solution.py:41
  592.9 1.0 copy-start.5
  647.4 110.5 %all-to-all-start.9 = ((f32[1,8,128,512]{3,2,0,1:T(8,128)}), f32[1,8,128,512]{3,2,0,1:T(8,128)}, u32[]{:S(2)}, u32[]{:S(2)}) async-start(f32[1,8,128,512]{3,2,0,1:T(8,128)} %bitcast.23), calls=%async_computation.9 | async-start | bytes 4194304 | tf_op jit(solution)/shard_map/all_to_all | solution.py:20
  651.8 105.0 %all-reduce.17.cloned.1.call-start = ((), (), s32[]{:S(2)}) async-start(), calls=%async_computation.18 | async-start | bytes 4194304 | tf_op jit(solution)/shard_map/psum | solution.py:99
  759.1 51.3 %all-to-all-start.10 = ((f32[4,2,128,256]{3,1,2,0:T(2,128)}), f32[4,2,128,256]{3,1,2,0:T(2,128)}, u32[]{:S(2)}, u32[]{:S(2)}) async-start(f32[4,2,128,256]{3,1,2,0:T(2,128)} %broadcast_in_dim.21), calls=%async_computation.10 | async-start | bytes 2097152 | tf_op jit(solution)/shard_map/all_to_all | solution.py:42
  763.4 116.4 %all-reduce.23.cloned.1.call-start = ((), (), s32[]{:S(2)}) async-start(), calls=%async_computation.21 | async-start | bytes 4194304 | tf_op jit(solution)/shard_map/psum | solution.py:110
  812.8 67.0 %copy-start.6 = (f32[128,2048]{1,0:T(8,128)S(1)}, f32[128,2048]{1,0:T(8,128)}, u32[]{:S(2)}) copy-start(f32[128,2048]{1,0:T(8,128)} %copy-done.5) | copy-start | bytes 3145732
  812.8 30.2 %all-to-all-start.11 = ((f32[1,8,128,256]{3,2,0,1:T(8,128)}), f32[1,8,128,256]{3,2,0,1:T(8,128)S(1)}, u32[]{:S(2)}, u32[]{:S(2)}) async-start(f32[1,8,128,256]{3,2,0,1:T(8,128)} %bitcast.107), calls=%async_computation.11 | async-start | bytes 2097152 | tf_op jit(solution)/shard_map/all_to_all | solution.py:41
  882.4 1.0 copy-start.7
  882.5 59.4 %copy-start.2 = (f32[128,2048]{1,0:T(8,128)}, f32[128,2048]{1,0:T(8,128)S(1)}, u32[]{:S(2)}) copy-start(f32[128,2048]{1,0:T(8,128)S(1)} %get-tuple-element.12) | copy-start | bytes 3145732
  936.9 110.7 %all-to-all-start.13 = ((f32[1,8,128,512]{3,2,0,1:T(8,128)}), f32[1,8,128,512]{3,2,0,1:T(8,128)}, u32[]{:S(2)}, u32[]{:S(2)}) async-start(f32[1,8,128,512]{3,2,0,1:T(8,128)} %bitcast.34), calls=%async_computation.13 | async-start | bytes 4194304 | tf_op jit(solution)/shard_map/all_to_all | solution.py:20
  941.4 105.3 %all-reduce.19.cloned.1.call-start = ((), (), s32[]{:S(2)}) async-start(), calls=%async_computation.19 | async-start | bytes 4194304 | tf_op jit(solution)/shard_map/psum | solution.py:99
  1048.9 50.7 %all-to-all-start.14 = ((f32[4,2,128,256]{3,1,2,0:T(2,128)}), f32[4,2,128,256]{3,1,2,0:T(2,128)S(1)}, u32[]{:S(2)}, u32[]{:S(2)}) async-start(f32[4,2,128,256]{3,1,2,0:T(2,128)} %broadcast_in_dim.23), calls=%async_computation.14 | async-start | bytes 2097152 | tf_op jit(solution)/shard_map/all_to_all | solution.py:42
  1052.6 116.5 %all-reduce.21.cloned.1.call-start = ((), (), s32[]{:S(2)}) async-start(), calls=%async_computation.20 | async-start | bytes 4194304 | tf_op jit(solution)/shard_map/psum | solution.py:110
  1100.6 68.4 %copy-start.3 = (f32[128,2048]{1,0:T(8,128)S(1)}, f32[128,2048]{1,0:T(8,128)}, u32[]{:S(2)}) copy-start(f32[128,2048]{1,0:T(8,128)} %copy-done.2) | copy-start | bytes 3145732
  1100.6 68.4 %copy-start.8 = (f32[128,2048]{1,0:T(8,128)S(1)}, f32[128,2048]{1,0:T(8,128)}, u32[]{:S(2)}) copy-start(f32[128,2048]{1,0:T(8,128)} %copy-done.7) | copy-start | bytes 3145732
  1100.7 30.2 %all-to-all-start.15 = ((f32[1,8,128,256]{3,2,0,1:T(8,128)}), f32[1,8,128,256]{3,2,0,1:T(8,128)S(1)}, u32[]{:S(2)}, u32[]{:S(2)}) async-start(f32[1,8,128,256]{3,2,0,1:T(8,128)} %bitcast.105), calls=%async_computation.15 | async-start | bytes 2097152 | tf_op jit(solution)/shard_map/all_to_all | solution.py:41
Sparse Core Ops, SparseCore 0:
  110.4 64.4 all-reduce.12
  402.6 64.4 all-reduce.14
  692.3 64.4 all-reduce.16
  982.1 64.5 all-reduce.18
Sparse Core Ops, SparseCore 1:
  228.5 69.2 all-reduce.26
  521.0 69.2 all-reduce.24
  810.5 69.2 all-reduce.22
  1099.6 69.3 all-reduce.20
